TPU v7x, 32 devices: a whole 2x2x4 slice. The times are simulated.
32 devices in a mesh: seq: 8 (over z, y), dp: 4 (over x, core).
Axes of the slice: x: 2, y: 2, z: 4, core: 2. Of those that a mesh axis runs over, the one named last changes fastest.
Arguments:
- tokens: bfloat16 [4, 2048, 2048], P('dp', 'seq'), may hold values from -6 to 6
- query_weight: bfloat16 [2048, 2048], P(None, 'seq'), may hold values from -0.125 to 0.125
- key_rows: bfloat16 [4, 2048, 2048], P('dp', 'seq'), may hold values from -6 to 6
- value_rows: bfloat16 [4, 2048, 2048], P('dp', 'seq'), may hold values from -6 to 6
- out_grad: bfloat16 [4, 2048, 2048], P('dp', 'seq'), may hold values from -6 to 6
Outputs:
- attended: bfloat16 [4, 2048, 2048], P('dp', 'seq')
- key_grad: bfloat16 [4, 2048, 2048], P('dp', 'seq')
- value_grad: bfloat16 [4, 2048, 2048], P('dp', 'seq')
- weight_grad: float32 [2048, 2048], P('seq')
All inputs are finite; a program needn't handle non-finite values.
Results may differ from a plain program's by a relative error of at most 0.0058.
Values may be sent and summed in bfloat16 or wider, within the bound.
No kernel may reach another device: no remote copies, remote signals or barrier semaphores. Data moves between devices by JAX's collectives and lax.ppermute only.
A program may use at most 320 MiB of HBM per device.

v0:
```python
import math
import jax
import jax.numpy as jnp
from jax import lax
from jax.sharding import PartitionSpec as P

DH = 128


def carried_in(value, axis, join, neutral, backward):
    count, mine = (lax.axis_size(axis), lax.axis_index(axis))
    pieces = lax.all_gather(value, axis)
    if backward:
        pieces = pieces[::-1]
        mine = count - 1 - mine
    total = jnp.full_like(value, 0) + jnp.asarray(neutral, value.dtype)

    def step(position, total):
        longer = join(total, pieces[position])
        return jnp.where(position < mine, longer, total)

    return lax.fori_loop(0, count - 1, step, total)


def pair_sum(earlier, later):
    return jax.tree.map(jnp.add, earlier, later)


def body(tokens, query_weight, key_rows, value_rows, out_grad):
    row_count = tokens.shape[1]
    hidden_width = key_rows.shape[2]
    head_count = hidden_width // DH
    seq_count = lax.axis_size("seq")
    factor = 1.0 / math.sqrt(DH * row_count * seq_count)
    local_tokens = tokens[0]
    query_rows = jnp.dot(
        local_tokens,
        lax.all_gather(query_weight, "seq", axis=1, tiled=True),
        preferred_element_type=jnp.float32,
    ).astype(jnp.bfloat16)
    query_heads = query_rows.reshape(row_count, head_count, DH)
    key_heads = key_rows[0].reshape(row_count, head_count, DH)
    value_heads = value_rows[0].reshape(row_count, head_count, DH)
    grad_heads = out_grad[0].reshape(row_count, head_count, DH)
    block_kv = jnp.einsum(
        "rhd,rhe->hde", key_heads, value_heads, preferred_element_type=jnp.float32
    )
    block_qg = jnp.einsum(
        "rhd,rhe->hde", query_heads, grad_heads, preferred_element_type=jnp.float32
    )
    zero_state = jnp.zeros_like(block_kv)
    prefix_state = carried_in(block_kv, "seq", pair_sum, zero_state, False)
    suffix_state = carried_in(block_qg, "seq", pair_sum, zero_state, True)
    prefix_half = prefix_state.astype(jnp.bfloat16)
    suffix_half = suffix_state.astype(jnp.bfloat16)
    lower_mask = (
        lax.broadcasted_iota(jnp.int32, (row_count, row_count), 0)
        >= lax.broadcasted_iota(jnp.int32, (row_count, row_count), 1)
    )[None]
    key_scores = jnp.where(
        lower_mask,
        factor
        * jnp.einsum("ihd,jhd->hij", query_heads, key_heads, preferred_element_type=jnp.float32),
        0.0,
    ).astype(jnp.bfloat16)
    grad_scores = jnp.where(
        lower_mask,
        factor
        * jnp.einsum("ihe,jhe->hij", grad_heads, value_heads, preferred_element_type=jnp.float32),
        0.0,
    ).astype(jnp.bfloat16)
    attended = jnp.einsum(
        "hij,jhe->ihe", key_scores, value_heads, preferred_element_type=jnp.float32
    ) + factor * jnp.einsum(
        "ihd,hde->ihe", query_heads, prefix_half, preferred_element_type=jnp.float32
    )
    query_grad = jnp.einsum(
        "hij,jhd->ihd", grad_scores, key_heads, preferred_element_type=jnp.float32
    ) + factor * jnp.einsum(
        "ihe,hde->ihd", grad_heads, prefix_half, preferred_element_type=jnp.float32
    )
    key_grad = jnp.einsum(
        "hij,ihd->jhd", grad_scores, query_heads, preferred_element_type=jnp.float32
    ) + factor * jnp.einsum(
        "jhe,hde->jhd", value_heads, suffix_half, preferred_element_type=jnp.float32
    )
    value_grad = jnp.einsum(
        "hij,ihe->jhe", key_scores, grad_heads, preferred_element_type=jnp.float32
    ) + factor * jnp.einsum(
        "jhd,hde->jhe", key_heads, suffix_half, preferred_element_type=jnp.float32
    )
    attended = attended.reshape(1, row_count, hidden_width).astype(jnp.bfloat16)
    query_grad = query_grad.reshape(row_count, hidden_width).astype(jnp.bfloat16)
    key_grad = key_grad.reshape(1, row_count, hidden_width).astype(jnp.bfloat16)
    value_grad = value_grad.reshape(1, row_count, hidden_width).astype(jnp.bfloat16)
    grad_shard = lax.psum_scatter(
        lax.dot_general(
            local_tokens, query_grad, (((0,), (0,)), ((), ())), preferred_element_type=jnp.float32
        ),
        "seq",
        scatter_dimension=0,
        tiled=True,
    )
    weight_grad = lax.psum(grad_shard, "dp")
    return (attended, key_grad, value_grad, weight_grad)


def solution(mesh):
    return jax.shard_map(
        body,
        mesh=mesh,
        in_specs=(
            P("dp", "seq", None),
            P(None, "seq"),
            P("dp", "seq", None),
            P("dp", "seq", None),
            P("dp", "seq", None),
        ),
        out_specs=(
            P("dp", "seq", None),
            P("dp", "seq", None),
            P("dp", "seq", None),
            P("seq", None),
        ),
        check_vma=False,
    )
```

profile of v0, /device:TPU:0, one launch (start us, length us, event | category | flops | bytes accessed | tf_op | source)
XLA Modules:
  0.0 732.2 jit_solution(10739160041827640124)
XLA Ops:
  13.8 2.5 copy.58
  16.3 121.4 %all-gather.6.cloned.1.call-done = bf16[2048,2048]{1,0:T(8,128)(2,1)} async-done(((bf16[2048,256]{1,0:T(8,128)(2,1)}), bf16[2048,2048]{1,0:T(8,128)(2,1)}) %all-gather.6.cloned.1.call-update) | async-done | bytes 8388624 | tf_op jit(solution)/shard_map/all_gather | solution.py:38
  137.7 6.7 convolution_convert_fusion
  145.9 3.2 fusion.11
  149.3 2.1 select_convert_fusion
  152.8 2.2 fusion.24
  155.0 108.1 %all-gather.8.cloned.1.call-done = f32[128,128,128]{2,1,0:T(8,128)} async-done(((f32[16,128,128]{2,1,0:T(8,128)}), f32[128,128,128]{2,1,0:T(8,128)}) %all-gather.8.cloned.1.call-update) | async-done | bytes 8388624 | tf_op jit(solution)/shard_map/all_gather | solution.py:12
  263.1 11.6 %while.28 = (s32[]{:T(128)}, f32[16,128,128]{2,1,0:T(8,128)S(1)}, s32[]{:T(128)}, f32[8,16,128,128]{3,2,1,0:T(8,128)}, s32[]{:T(128)}, /*index=5*/s32[]{:T(128)}) while((s32[]{:T(128)}, f32[16,128,128]{2,1,0:T(8,128)S(1)}, s32[]{:T(128)}, f32[8,16,128,128]{3,2,1,0:T(8,128)}, s32[]{:T(128)}, /*index=5*/s32[]{:T(128)}) %tuple.81), condition=%wide.region_1.2_spmd.clone, body=%wide.region_0.1_spmd.clone.sunk | while | flops 786436 | bytes 3145821 | solution.py:22
  269.6 1.7 add_select_fusion.4
  271.3 1.7 add_select_fusion.4
  273.0 1.7 add_select_fusion.4
  274.8 2.4 fusion
  277.2 8.1 %convolution_bitcast_fusion = f32[2048,2048]{0,1:T(8,128)} fusion(bf16[256,2048]{0,1:T(8,128)(2,1)S(1)} %bitcast.79, bf16[1,256,2048]{2,1,0:T(8,128)(2,1)S(1)} %copy-done), kind=kOutput, calls=%fused_computation.2 | convolution fusion | flops 2147483648 | bytes 18874368 | tf_op jit(solution)/shard_map/dot_general | solution.py:97
  285.6 2.4 select_convert_fusion.1
  291.5 2.4 copy.49
  293.8 3.4 fusion.23
  297.2 90.8 %all-gather.10.cloned.1.call-done = f32[128,128,128]{2,1,0:T(8,128)} async-done(((f32[16,128,128]{2,1,0:T(8,128)}), f32[128,128,128]{2,1,0:T(8,128)}) %all-gather.10.cloned.1.call-update) | async-done | bytes 8388624 | tf_op jit(solution)/shard_map/all_gather | solution.py:12
  387.9 7.7 %rev.3 = f32[8,16,128,128]{3,2,1,0:T(8,128)} reverse(f32[8,16,128,128]{3,2,1,0:T(8,128)} %bitcast.78), dimensions={0} | reverse | bytes 16777216 | tf_op jit(solution)/shard_map/rev | solution.py:14
  395.7 11.4 %while.29 = (s32[]{:T(128)}, f32[16,128,128]{2,1,0:T(8,128)S(1)}, s32[]{:T(128)}, f32[8,16,128,128]{3,2,1,0:T(8,128)}, s32[]{:T(128)}, /*index=5*/s32[]{:T(128)}) while((s32[]{:T(128)}, f32[16,128,128]{2,1,0:T(8,128)S(1)}, s32[]{:T(128)}, f32[8,16,128,128]{3,2,1,0:T(8,128)}, s32[]{:T(128)}, /*index=5*/s32[]{:T(128)}) %tuple.68), condition=%wide.region_3.4_spmd.clone, body=%wide.region_2.3_spmd.clone.sunk | while | flops 786436 | bytes 3145821 | solution.py:22
  407.1 263.0 %reduce-scatter.2.cloned.1.call-done = f32[256,2048]{0,1:T(8,128)} async-done(((f32[2048,2048]{0,1:T(8,128)}), f32[256,2048]{0,1:T(8,128)}) %reduce-scatter.2.cloned.1.call-update) | async-done | bytes 2097168 | tf_op jit(solution)/shard_map/reduce_scatter | solution.py:96
  670.1 3.1 add_convert_fusion
  673.2 2.4 copy.50
  679.9 43.0 %all-reduce.2.cloned.1.call-done = f32[256,2048]{0,1:T(8,128)} async-done(((f32[256,2048]{0,1:T(8,128)}), f32[256,2048]{0,1:T(8,128)}) %all-reduce.2.cloned.1.call-update) | async-done | bytes 2097168 | tf_op jit(solution)/shard_map/psum | solution.py:104
  722.8 2.9 copy.52
  (60 shorter events, 35.0 us)
Async XLA Ops:
  7.2 130.6 %copy-start = (bf16[1,256,2048]{2,1,0:T(8,128)(2,1)S(1)}, bf16[1,256,2048]{2,1,0:T(8,128)(2,1)}, u32[]{:S(2)}) copy-start(bf16[1,256,2048]{2,1,0:T(8,128)(2,1)} %param.9) | copy-start | bytes 3145732
  7.2 2.3 copy-start.12
  7.2 130.5 %all-gather.6.cloned.1.call-start = ((), (), s32[]{:S(2)}) async-start(), calls=%async_computation.1 | async-start | bytes 9437184 | tf_op jit(solution)/shard_map/all_gather | solution.py:38
  7.9 255.2 %all-gather.8.cloned.1.call-start = ((), (), s32[]{:S(2)}) async-start(), calls=%async_computation.4 | async-start | bytes 9437184 | tf_op jit(solution)/shard_map/all_gather | solution.py:12
  12.3 1.5 copy-start.6
  13.8 374.2 %all-gather.10.cloned.1.call-start = ((), (), s32[]{:S(2)}) async-start(), calls=%async_computation.5 | async-start | bytes 9437184 | tf_op jit(solution)/shard_map/all_gather | solution.py:12
  145.9 3.3 copy-start.2
  149.2 520.9 %reduce-scatter.2.cloned.1.call-start = ((), (), s32[]{:S(2)}) async-start(), calls=%async_computation.2 | async-start | bytes 18874368 | tf_op jit(solution)/shard_map/reduce_scatter | solution.py:96
  149.3 3.5 copy-start.7
  151.5 1.3 copy-start.11
  285.3 437.5 %all-reduce.2.cloned.1.call-start = ((), (), s32[]{:S(2)}) async-start(), calls=%async_computation.3 | async-start | bytes 4194304 | tf_op jit(solution)/shard_map/psum | solution.py:104
  288.0 1.4 copy-start.9
  288.0 2.0 copy-start.3
  291.5 2.4 copy-start.4
  673.2 2.4 copy-start.8
  675.5 1.3 copy-start.5
  675.5 2.3 copy-start.10
  678.4 47.3 %copy-start.1 = (bf16[1,256,2048]{2,1,0:T(8,128)(2,1)S(1)}, bf16[1,256,2048]{2,1,0:T(8,128)(2,1)}, u32[]{:S(2)}) copy-start(bf16[1,256,2048]{2,1,0:T(8,128)(2,1)} %param.9) | copy-start | bytes 3145732
Sparse Core Ops, SparseCore 0:
  10.0 127.6 all-gather.5
  140.4 122.6 all-gather.7
  265.3 122.6 all-gather.9
  391.6 278.4 reduce-scatter.1
  672.3 50.4 all-reduce.1
where the time goes:
time: 733 us; the launch traced here: 732 us
  waiting for transfers between devices  627 us (86%)
  matrix products  38.5 us (5%)
  local copies, waits for them, and re-layouts  29.3 us (4%)
  other arithmetic  22.7 us (3%)
  between operations  14 us (2%)
    reduce_scatter x1, waiting for transfers between devices, body(): lax.psum_scatter(lax.dot_general(local_tokens, query_grad, (((0,), (0,)),...  263 us
    all_gather x2, waiting for transfers between devices, carried_in(): pieces = lax.all_gather(value, axis)  199 us
    all_gather x1, waiting for transfers between devices, body(): lax.all_gather(query_weight, 'seq', axis=1, tiled=True)  121 us
    psum x1, waiting for transfers between devices, body(): weight_grad = lax.psum(grad_shard, 'dp')  43 us
    select_n x14, other arithmetic, step(): return jnp.where(position < mine, longer, total)  22.7 us
    unnamed x33, local copies, waits for them, and re-layouts  18.5 us
  transfers between devices with their start and end apart: 5, of which 5 were waited for; matrix products, arithmetic and copies ran while one was open for 11% of the time, Pallas kernels for 0%

commit v1 on v0

--- a/solution.py
+++ b/solution.py
@@ -101,7 +101,7 @@
         scatter_dimension=0,
         tiled=True,
     )
-    weight_grad = lax.psum(grad_shard, "dp")
+    weight_grad = jnp.sum(lax.all_gather(grad_shard, "dp"), axis=0)
     return (attended, key_grad, value_grad, weight_grad)
 
 

time: 733 us -> 767 us (1.046)
  other arithmetic: 22.7 us -> 36.7 us
  local copies, waits for them, and re-layouts: 29.3 us -> 40.5 us
  waiting for transfers between devices: 627 us -> 635 us
    psum x1 -> x0, waiting for transfers between devices: 43 us -> none  [body(): weight_grad = lax.psum(grad_shard, 'dp')]
    all_gather x2, waiting for transfers between devices: 199 us -> 232 us  [carried_in(): pieces = lax.all_gather(value, axis)]
    all_gather x0 -> x1, waiting for transfers between devices: none -> 28.3 us  [body(): weight_grad = jnp.sum(lax.all_gather(grad_shard, 'dp'), axis=0)]
    all_gather x1, waiting for transfers between devices: 121 us -> 103 us  [body(): lax.all_gather(query_weight, 'seq', axis=1, tiled=True)]
    reduce_sum x0 -> x1, other arithmetic: none -> 13.8 us  [body(): weight_grad = jnp.sum(lax.all_gather(grad_shard, 'dp'), axis=0)]
    all_gather x0 -> x1, local copies, waits for them, and re-layouts: none -> 10.5 us  [body(): weight_grad = jnp.sum(lax.all_gather(grad_shard, 'dp'), axis=0)]
  transfers between devices with their start and end apart: 5 -> 5, of which waited for: 5 -> 5; matrix products, arithmetic and copies ran while one was open for 11% -> 10% of each run, Pallas kernels for 0% -> 0%
where the time goes in v1:
time: 767 us; the launch traced here: 765 us
  waiting for transfers between devices  635 us (83%)
  local copies, waits for them, and re-layouts  40.5 us (5%)
  matrix products  38.8 us (5%)
  other arithmetic  36.7 us (5%)
  between operations  14 us (2%)
    reduce_scatter x1, waiting for transfers between devices, body(): lax.psum_scatter(lax.dot_general(local_tokens, query_grad, (((0,), (0,)),...  271 us
    all_gather x2, waiting for transfers between devices, carried_in(): pieces = lax.all_gather(value, axis)  232 us
    all_gather x1, waiting for transfers between devices, body(): lax.all_gather(query_weight, 'seq', axis=1, tiled=True)  103 us
    all_gather x1, waiting for transfers between devices, body(): weight_grad = jnp.sum(lax.all_gather(grad_shard, 'dp'), axis=0)  28.3 us
    select_n x14, other arithmetic, step(): return jnp.where(position < mine, longer, total)  22.8 us
    unnamed x33, local copies, waits for them, and re-layouts  18.2 us
  transfers between devices with their start and end apart: 5, of which 5 were waited for; matrix products, arithmetic and copies ran while one was open for 10% of the time, Pallas kernels for 0%

profile of v1, /device:TPU:0, one launch (start us, length us, event | category | flops | bytes accessed | tf_op | source)
XLA Modules:
  0.0 765.3 jit_solution(17214335834725478975)
XLA Ops:
  14.0 2.5 copy.57
  16.5 2.1 select_convert_fusion
  20.0 2.2 fusion.24
  22.2 118.3 %all-gather.10.cloned.1.call-done = f32[128,128,128]{2,1,0:T(8,128)} async-done(((f32[16,128,128]{2,1,0:T(8,128)}), f32[128,128,128]{2,1,0:T(8,128)}) %all-gather.10.cloned.1.call-update) | async-done | bytes 8388624 | tf_op jit(solution)/shard_map/all_gather | solution.py:12
  140.5 11.5 %while.28 = (s32[]{:T(128)}, f32[16,128,128]{2,1,0:T(8,128)S(1)}, s32[]{:T(128)}, f32[8,16,128,128]{3,2,1,0:T(8,128)}, s32[]{:T(128)}, /*index=5*/s32[]{:T(128)}) while((s32[]{:T(128)}, f32[16,128,128]{2,1,0:T(8,128)S(1)}, s32[]{:T(128)}, f32[8,16,128,128]{3,2,1,0:T(8,128)}, s32[]{:T(128)}, /*index=5*/s32[]{:T(128)}) %tuple.81), condition=%wide.region_1.2_spmd.clone, body=%wide.region_0.1_spmd.clone.sunk | while | flops 786436 | bytes 3145821 | solution.py:22
  152.1 2.5 fusion
  154.6 8.1 %convolution_bitcast_fusion = f32[2048,2048]{0,1:T(8,128)} fusion(bf16[256,2048]{0,1:T(8,128)(2,1)S(1)} %bitcast.81, bf16[1,256,2048]{2,1,0:T(8,128)(2,1)S(1)} %copy-done), kind=kOutput, calls=%fused_computation.2 | convolution fusion | flops 2147483648 | bytes 18874368 | tf_op jit(solution)/shard_map/dot_general | solution.py:97
  162.7 103.0 %all-gather.8.cloned.1.call-done = bf16[2048,2048]{1,0:T(8,128)(2,1)} async-done(((bf16[2048,256]{1,0:T(8,128)(2,1)}), bf16[2048,2048]{1,0:T(8,128)(2,1)}) %all-gather.8.cloned.1.call-update) | async-done | bytes 8388624 | tf_op jit(solution)/shard_map/all_gather | solution.py:38
  265.7 6.7 convolution_convert_fusion
  273.9 3.3 fusion.11
  277.4 270.6 %reduce-scatter.2.cloned.1.call-done = f32[256,2048]{0,1:T(8,128)} async-done(((f32[2048,2048]{0,1:T(8,128)}), f32[256,2048]{0,1:T(8,128)}) %reduce-scatter.2.cloned.1.call-update) | async-done | bytes 2097168 | tf_op jit(solution)/shard_map/reduce_scatter | solution.py:96
  548.1 2.4 select_convert_fusion.1
  554.0 2.4 copy.48
  556.3 3.6 fusion.23
  559.9 113.7 %all-gather.12.cloned.1.call-done = f32[128,128,128]{2,1,0:T(8,128)} async-done(((f32[16,128,128]{2,1,0:T(8,128)}), f32[128,128,128]{2,1,0:T(8,128)}) %all-gather.12.cloned.1.call-update) | async-done | bytes 8388624 | tf_op jit(solution)/shard_map/all_gather | solution.py:12
  673.6 8.6 %rev.3 = f32[8,16,128,128]{3,2,1,0:T(8,128)} reverse(f32[8,16,128,128]{3,2,1,0:T(8,128)} %bitcast.80), dimensions={0} | reverse | bytes 16777216 | tf_op jit(solution)/shard_map/rev | solution.py:14
  682.2 11.6 %while.29 = (s32[]{:T(128)}, f32[16,128,128]{2,1,0:T(8,128)S(1)}, s32[]{:T(128)}, f32[8,16,128,128]{3,2,1,0:T(8,128)}, s32[]{:T(128)}, /*index=5*/s32[]{:T(128)}) while((s32[]{:T(128)}, f32[16,128,128]{2,1,0:T(8,128)S(1)}, s32[]{:T(128)}, f32[8,16,128,128]{3,2,1,0:T(8,128)}, s32[]{:T(128)}, /*index=5*/s32[]{:T(128)}) %tuple.68), condition=%wide.region_3.4_spmd.clone, body=%wide.region_2.3_spmd.clone.sunk | while | flops 786436 | bytes 3145821 | solution.py:22
  682.2 1.7 add_select_fusion.5
  693.9 3.1 add_convert_fusion
  696.9 2.4 copy.49
  703.3 28.3 %all-gather.14.cloned.1.call-done = f32[1024,2048]{0,1:T(8,128)} async-done(((f32[256,2048]{0,1:T(8,128)}), f32[1024,2048]{0,1:T(8,128)}) %all-gather.14.cloned.1.call-update) | async-done | bytes 8388624 | tf_op jit(solution)/shard_map/all_gather | solution.py:104
  731.5 10.5 %reshape.65 = f32[4,256,2048]{1,0,2:T(4,128)} reshape(f32[1024,2048]{0,1:T(8,128)} %all-gather.14.cloned.1.call-done) | data formatting | bytes 16777216 | tf_op jit(solution)/shard_map/all_gather | solution.py:104
  742.1 13.8 %reduce_sum.9 = f32[256,2048]{0,1:T(8,128)} reduce(f32[4,256,2048]{1,0,2:T(4,128)} %reshape.65, f32[]{:T(128)} %constant.55.clone.1), dimensions={0}, to_apply=%region_5.6 | reduce | flops 1572864 | bytes 10485764 | tf_op jit(solution)/shard_map/reduce_sum | solution.py:104
  755.9 2.9 copy.51
  (62 shorter events, 38.4 us)
Async XLA Ops:
  7.2 147.4 %copy-start = (bf16[1,256,2048]{2,1,0:T(8,128)(2,1)S(1)}, bf16[1,256,2048]{2,1,0:T(8,128)(2,1)}, u32[]{:S(2)}) copy-start(bf16[1,256,2048]{2,1,0:T(8,128)(2,1)} %param.9) | copy-start | bytes 3145732
  7.2 1.7 copy-start.12
  7.2 133.3 %all-gather.10.cloned.1.call-start = ((), (), s32[]{:S(2)}) async-start(), calls=%async_computation.3 | async-start | bytes 9437184 | tf_op jit(solution)/shard_map/all_gather | solution.py:12
  11.7 1.5 copy-start.6
  13.2 252.5 %all-gather.8.cloned.1.call-start = ((), (), s32[]{:S(2)}) async-start(), calls=%async_computation.1 | async-start | bytes 9437184 | tf_op jit(solution)/shard_map/all_gather | solution.py:38
  14.0 534.1 %reduce-scatter.2.cloned.1.call-start = ((), (), s32[]{:S(2)}) async-start(), calls=%async_computation.2 | async-start | bytes 18874368 | tf_op jit(solution)/shard_map/reduce_scatter | solution.py:96
  16.5 3.5 copy-start.7
  18.7 1.3 copy-start.11
  162.7 511.0 %all-gather.12.cloned.1.call-start = ((), (), s32[]{:S(2)}) async-start(), calls=%async_computation.4 | async-start | bytes 9437184 | tf_op jit(solution)/shard_map/all_gather | solution.py:12
  273.9 3.3 copy-start.2
  277.2 454.3 %all-gather.14.cloned.1.call-start = ((), (), s32[]{:S(2)}) async-start(), calls=%async_computation.5 | async-start | bytes 10485760 | tf_op jit(solution)/shard_map/all_gather | solution.py:104
  550.5 1.4 copy-start.9
  550.5 2.0 copy-start.3
  554.0 2.4 copy-start.4
  696.9 2.4 copy-start.8
  699.3 1.2 copy-start.5
  699.3 1.9 copy-start.10
  742.1 16.7 %copy-start.1 = (bf16[1,256,2048]{2,1,0:T(8,128)(2,1)S(1)}, bf16[1,256,2048]{2,1,0:T(8,128)(2,1)}, u32[]{:S(2)}) copy-start(bf16[1,256,2048]{2,1,0:T(8,128)(2,1)} %param.9) | copy-start | bytes 3145732
Sparse Core Ops, SparseCore 0:
  13.3 127.1 all-gather.9
  142.6 123.1 all-gather.7
  269.5 278.4 reduce-scatter.1
  550.0 123.5 all-gather.11
  675.0 56.4 all-gather.13
